TPU v7x, 512 devices: a whole 4x4x16 slice. The times are simulated.
512 devices in a mesh: ctx: 32 (over x, z_lo), tp: 16 (over y, z_hi, core).
Axes of the slice: x: 4, y: 4, z: 16 (z_hi: 2, z_lo: 8; z = z_hi * 8 + z_lo), core: 2. Of those that a mesh axis runs over, the one named last changes fastest.
Arguments:
- queries: bfloat16 [4096, 4096], P('ctx', 'tp'), may hold values from -5 to 5
- key_states: bfloat16 [4096, 4096], P('ctx', 'tp'), may hold values from -5 to 5
- value_states: bfloat16 [4096, 4096], P('ctx', 'tp'), may hold values from -6 to 6
- attn_output: bfloat16 [4096, 4096], P('ctx', 'tp'), may hold values from -6 to 6
- output_grad: bfloat16 [4096, 4096], P('ctx', 'tp'), may hold values from -6 to 6
- block_map: int32 [32, 32], replicated, may hold values from 0 to 1, as said below
- w_query: bfloat16 [8192, 4096], P('ctx', 'tp'), may hold values from -0.09375 to 0.09375
- w_key: bfloat16 [8192, 4096], P('ctx', 'tp'), may hold values from -0.09375 to 0.09375
- w_value: bfloat16 [8192, 4096], P('ctx', 'tp'), may hold values from -0.09375 to 0.09375
Outputs:
- grad_input: bfloat16 [4096, 8192], P('tp', 'ctx')
Inputs may be any that keep to these rules, and one draw needn't show every extreme that they name: block_map[i, j] is 1 wherever |i - j| <= 1; elsewhere each row is 1 on a share of its entries that differs from row to row.
All inputs are finite; a program needn't handle non-finite values.
Results may differ from a plain program's by a relative error of at most 0.014.
Values may be sent and summed in bfloat16 or wider, within the bound.
No kernel may reach another device: no remote copies, remote signals or barrier semaphores. Data moves between devices by JAX's collectives and lax.ppermute only.
A program may use at most 64 MiB of HBM per device.

v0:
```python
import math
import jax
import jax.numpy as jnp
from jax import lax
from jax.sharding import PartitionSpec as P

HD = 128
BLK = 128
NEG_FILL = -1e30


def block_mask(block_map, row_offset, row_count, col_offset, col_count):
    tiles = lax.dynamic_slice(
        block_map, (row_offset // BLK, col_offset // BLK), (row_count // BLK, col_count // BLK)
    )
    spread = jnp.broadcast_to(
        tiles[:, None, :, None], (row_count // BLK, BLK, col_count // BLK, BLK)
    )
    return spread.reshape(row_count, col_count) > 0


def resolved_rows(values):
    return lax.optimization_barrier(values.astype(jnp.bfloat16)).astype(jnp.float32)


def stat_update(state, query_heads, key_block, allowed, score_scale):
    row_max, row_sum = state
    scores = (
        jnp.einsum("qhd,khd->hqk", query_heads, key_block, preferred_element_type=jnp.float32)
        * score_scale
    )
    masked = jnp.where(allowed[None], scores, NEG_FILL)
    new_max = jnp.maximum(row_max, jnp.max(masked, axis=2))
    kept = jnp.where(allowed[None], jnp.exp(masked - new_max[:, :, None]), 0.0)
    return (new_max, row_sum * jnp.exp(row_max - new_max) + jnp.sum(kept, axis=2))


def gradient_block(
    query_heads, grad_heads, key_block, value_block, log_total, row_delta, allowed, score_scale
):
    scores = (
        jnp.einsum("qhd,khd->hqk", query_heads, key_block, preferred_element_type=jnp.float32)
        * score_scale
    )
    masked = jnp.where(allowed[None], scores, NEG_FILL)
    probs = jnp.where(allowed[None], jnp.exp(masked - log_total[:, :, None]), 0.0)
    probs_low = probs.astype(jnp.bfloat16)
    dprobs = jnp.einsum("qhd,khd->hqk", grad_heads, value_block, preferred_element_type=jnp.float32)
    score_gradient = (probs * (dprobs - row_delta[:, :, None]) * score_scale).astype(jnp.bfloat16)
    return (probs_low, score_gradient)


def per_device(
    queries, key_states, value_states, attn_output, output_grad, block_map, w_query, w_key, w_value
):
    slab_rows, width = queries.shape
    head_count = width // HD
    context_count = lax.axis_size("ctx")
    score_scale = 1.0 / math.sqrt(HD)
    row_offset = lax.axis_index("ctx") * slab_rows
    query_heads = queries.reshape(slab_rows, head_count, HD)
    grad_heads = output_grad.reshape(slab_rows, head_count, HD)
    output_heads = attn_output.reshape(slab_rows, head_count, HD)
    row_delta = jnp.sum(grad_heads.astype(jnp.float32) * output_heads.astype(jnp.float32), axis=2).T
    start_state = (
        jnp.full((head_count, slab_rows), NEG_FILL, jnp.float32),
        jnp.zeros((head_count, slab_rows), jnp.float32),
    )
    key_value = jnp.concatenate([key_states, value_states], axis=1)
    spread = jnp.broadcast_to(key_value[None], (context_count,) + key_value.shape)
    gathered = lax.all_to_all(spread, "ctx", 0, 0, tiled=True).reshape(
        context_count * slab_rows, 2 * width
    )
    full_keys, full_values = (gathered[:, :width], gathered[:, width:])
    group_size = min(context_count, max(1, 512 // slab_rows))
    key_span = slab_rows * group_size
    total_block_count = context_count // group_size
    key_blocks = full_keys.reshape(total_block_count, key_span, head_count, HD)
    value_blocks = full_values.reshape(total_block_count, key_span, head_count, HD)
    block_ids = jnp.arange(total_block_count, dtype=jnp.int32)

    def stat_step(state, inputs):
        key_block, block_index = inputs
        allowed = block_mask(block_map, row_offset, slab_rows, block_index * key_span, key_span)

        def stat_active_step(previous):
            return stat_update(previous, query_heads, key_block, allowed, score_scale)

        return (
            lax.cond(jnp.any(allowed), stat_active_step, lambda previous: previous, state),
            None,
        )

    (row_max, row_sum), _ = lax.scan(stat_step, start_state, (key_blocks, block_ids))
    log_total = row_max + jnp.log(row_sum)

    def back_step(dq_total, inputs):
        key_block, value_block, block_index = inputs
        allowed = block_mask(block_map, row_offset, slab_rows, block_index * key_span, key_span)

        def back_active_step(previous):
            probs_low, score_gradient = gradient_block(
                query_heads,
                grad_heads,
                key_block,
                value_block,
                log_total,
                row_delta,
                allowed,
                score_scale,
            )
            dv_part = jnp.einsum(
                "hqk,qhd->khd", probs_low, grad_heads, preferred_element_type=jnp.float32
            ).astype(jnp.bfloat16)
            dk_part = jnp.einsum(
                "hqk,qhd->khd", score_gradient, query_heads, preferred_element_type=jnp.float32
            ).astype(jnp.bfloat16)
            per_slab = jnp.einsum(
                "hqgk,gkhd->gqhd",
                score_gradient.reshape(head_count, slab_rows, group_size, slab_rows),
                key_block.reshape(group_size, slab_rows, head_count, HD),
                preferred_element_type=jnp.float32,
            )
            joined = jnp.concatenate(
                [dk_part.reshape(key_span, width), dv_part.reshape(key_span, width)], axis=1
            )
            return (previous + jnp.sum(resolved_rows(per_slab), axis=0), joined)

        def empty_step(previous):
            return (previous, jnp.zeros((key_span, 2 * width), jnp.bfloat16))

        return lax.cond(jnp.any(allowed), back_active_step, empty_step, dq_total)

    dq_total, joined_blocks = lax.scan(
        back_step,
        jnp.zeros((slab_rows, head_count, HD), jnp.float32),
        (key_blocks, value_blocks, block_ids),
    )
    local_grads = dq_total.astype(jnp.bfloat16).reshape(slab_rows, width)
    part_grads = joined_blocks.reshape(context_count * slab_rows, 2 * width)
    part_width = part_grads.shape[1]
    arrived = lax.all_to_all(
        part_grads.reshape(context_count, slab_rows, part_width),
        "ctx",
        split_axis=0,
        concat_axis=0,
        tiled=True,
    )
    finished = jnp.sum(arrived.astype(jnp.float32), axis=0).astype(jnp.bfloat16)
    own_grads = jnp.concatenate([local_grads, finished], axis=1)
    gradients = lax.all_gather(own_grads, "ctx", axis=0, tiled=True)
    projections = jnp.concatenate([w_query, w_key, w_value], axis=1)
    return lax.psum_scatter(
        lax.dot_general(
            gradients, projections, (((1,), (1,)), ((), ())), preferred_element_type=jnp.float32
        ).astype(jnp.bfloat16),
        "tp",
        scatter_dimension=0,
        tiled=True,
    )


def solution(mesh):
    return jax.shard_map(
        per_device,
        mesh=mesh,
        in_specs=(
            P("ctx", "tp"),
            P("ctx", "tp"),
            P("ctx", "tp"),
            P("ctx", "tp"),
            P("ctx", "tp"),
            P(),
            P("ctx", "tp"),
            P("ctx", "tp"),
            P("ctx", "tp"),
        ),
        out_specs=P("tp", "ctx"),
        check_vma=False,
    )
```

profile of v0, /device:TPU:2, one launch (start us, length us, event | category | flops | bytes accessed | tf_op | source)
XLA Modules:
  0.0 892.0 jit_solution(6560580829469173553)
XLA Ops:
  6.5 0.9 pad_maximum_fusion.1
  7.5 2.9 broadcast_in_dim.103
  10.4 15.9 %all-to-all-start = ((bf16[32,128,512]{1,2,0:T(8,128)(2,1)}), bf16[32,128,512]{1,2,0:T(8,128)(2,1)}, u32[]{:S(2)}, u32[]{:S(2)}) async-start(bf16[32,128,512]{1,2,0:T(8,128)(2,1)} %broadcast_in_dim.103), calls=%async_computation | async-start | bytes 8388608 | tf_op jit(solution)/shard_map/all_to_all | solution.py:71
  26.9 174.6 %all-to-all-done = bf16[32,128,512]{1,2,0:T(8,128)(2,1)} async-done(((bf16[32,128,512]{1,2,0:T(8,128)(2,1)}), bf16[32,128,512]{1,2,0:T(8,128)(2,1)}, u32[]{:S(2)}, u32[]{:S(2)}) %all-to-all-start) | async-done | bytes 4194336 | tf_op jit(solution)/shard_map/all_to_all | solution.py:71
  201.5 6.5 copy.66
  208.0 3.8 fusion.27
  211.8 2.1 reshape.89
  213.9 2.0 copy.74
  215.9 30.8 %while.33 = (s32[]{:T(128)}, f32[2,128]{1,0:T(2,128)S(1)}, f32[2,128]{1,0:T(2,128)S(1)}, s32[8]{0:T(128)S(1)}, s32[32,32]{1,0:T(8,128)}, /*index=5*/s32[]{:T(128...) while((s32[]{:T(128)}, f32[2,128]{1,0:T(2,128)S(1)}, ...), condition=%wide.region_6.7_spmd, body=%wide.region_0.6_spmd.sunk | while | flops 34406940 | bytes 1391623 | solution.py:94
  220.9 0.8 broadcast_compare_fusion.6
  224.8 0.8 broadcast_compare_fusion.6
  228.6 0.8 broadcast_compare_fusion.6
  232.5 0.8 broadcast_compare_fusion.6
  236.3 0.8 broadcast_compare_fusion.6
  244.1 0.8 broadcast_compare_fusion.6
  246.7 4.0 reshape.90
  250.7 3.3 copy.75
  254.1 54.5 %while.34 = (s32[]{:T(128)}, f32[128,2,128]{2,0,1:T(8,128)S(1)}, bf16[8,512,512]{2,1,0:T(8,128)(2,1)}, s32[8]{0:T(128)S(1)}, s32[32,32]{1,0:T(8,128)}, /*index=5...) while((s32[]{:T(128)}, f32[128,2,128]{2,0,1:T(8,128)S(1)}, ...), condition=%wide.region_13.14_spmd, body=%wide.region_8.13_spmd.sunk | while | flops 170721312 | bytes 8655399 | solution.py:134
  257.4 2.5 conditional.5
  257.8 1.2 fusion.11
  260.1 0.8 constant_dynamic-update-slice_fusion.2
  264.2 2.5 conditional.5
  264.6 1.2 fusion.11
  266.9 0.8 constant_dynamic-update-slice_fusion.2
  271.0 2.5 conditional.5
  271.4 1.2 fusion.11
  273.7 0.8 constant_dynamic-update-slice_fusion.2
  277.8 2.5 conditional.5
  278.2 1.2 fusion.11
  280.5 0.8 constant_dynamic-update-slice_fusion.2
  284.6 2.5 conditional.5
  285.0 1.2 fusion.11
  287.3 0.8 constant_dynamic-update-slice_fusion.2
  291.4 2.5 conditional.5
  291.8 1.2 fusion.11
  294.1 0.9 constant_dynamic-update-slice_fusion.2
  298.2 2.5 conditional.5
  298.6 1.2 fusion.11
  300.9 0.8 constant_dynamic-update-slice_fusion.2
  305.0 2.5 conditional.5
  305.4 1.2 fusion.11
  307.7 0.8 constant_dynamic-update-slice_fusion.2
  308.5 18.0 %all-to-all-start.1 = ((bf16[32,128,512]{2,1,0:T(8,128)(2,1)}), bf16[32,128,512]{2,1,0:T(8,128)(2,1)}, u32[]{:S(2)}, u32[]{:S(2)}) async-start(bf16[32,128,512]{2,1,0:T(8,128)(2,1)} %bitcast.65), calls=%async_computation.1 | async-start | bytes 8388608 | tf_op jit(solution)/shard_map/all_to_all | solution.py:142
  326.8 175.0 %all-to-all-done.1 = bf16[32,128,512]{2,1,0:T(8,128)(2,1)} async-done(((bf16[32,128,512]{2,1,0:T(8,128)(2,1)}), bf16[32,128,512]{2,1,0:T(8,128)(2,1)}, u32[]{:S(2)}, u32[]{:S(2)}) %all-to-all-start.1) | async-done | bytes 4194336 | tf_op jit(solution)/shard_map/all_to_all | solution.py:142
  501.9 2.8 reduce_sum.43
  505.4 236.3 %all-gather.2.cloned.1.call-done = bf16[4096,768]{1,0:T(8,128)(2,1)} async-done(((bf16[128,768]{1,0:T(8,128)(2,1)}), bf16[4096,768]{1,0:T(8,128)(2,1)}) %all-gather.2.cloned.1.call-update) | async-done | bytes 6291472 | tf_op jit(solution)/shard_map/all_gather | solution.py:151
  741.7 6.0 convolution_convert_fusion.3
  747.7 137.5 %reduce-scatter.2.cloned.1.call-done = bf16[256,256]{1,0:T(8,128)(2,1)} async-done(((bf16[4096,256]{1,0:T(8,128)(2,1)}), bf16[256,256]{1,0:T(8,128)(2,1)}) %reduce-scatter.2.cloned.1.call-update) | async-done | bytes 131088 | tf_op jit(solution)/shard_map/reduce_scatter | solution.py:153
  (226 shorter events, 50.6 us)
Async XLA Ops:
  10.4 15.9 %copy-start.1 = (bf16[128,256]{1,0:T(8,128)(2,1)S(1)}, bf16[128,256]{1,0:T(8,128)(2,1)}, u32[]{:S(2)}) copy-start(bf16[128,256]{1,0:T(8,128)(2,1)} %param.17) | copy-start | bytes 196612
  10.4 16.2 %copy-start.2 = (bf16[128,256]{1,0:T(8,128)(2,1)S(1)}, bf16[128,256]{1,0:T(8,128)(2,1)}, u32[]{:S(2)}) copy-start(bf16[128,256]{1,0:T(8,128)(2,1)} %param.21) | copy-start | bytes 196612
  10.4 16.3 %copy-start = (bf16[128,256]{1,0:T(8,128)(2,1)S(1)}, bf16[128,256]{1,0:T(8,128)(2,1)}, u32[]{:S(2)}) copy-start(bf16[128,256]{1,0:T(8,128)(2,1)} %param.20) | copy-start | bytes 196612
  10.4 191.0 %all-to-all-start = ((bf16[32,128,512]{1,2,0:T(8,128)(2,1)}), bf16[32,128,512]{1,2,0:T(8,128)(2,1)}, u32[]{:S(2)}, u32[]{:S(2)}) async-start(bf16[32,128,512]{1,2,0:T(8,128)(2,1)} %broadcast_in_dim.103), calls=%async_computation | async-start | bytes 8388608 | tf_op jit(solution)/shard_map/all_to_all | solution.py:71
  308.5 193.3 %all-to-all-start.1 = ((bf16[32,128,512]{2,1,0:T(8,128)(2,1)}), bf16[32,128,512]{2,1,0:T(8,128)(2,1)}, u32[]{:S(2)}, u32[]{:S(2)}) async-start(bf16[32,128,512]{2,1,0:T(8,128)(2,1)} %bitcast.65), calls=%async_computation.1 | async-start | bytes 8388608 | tf_op jit(solution)/shard_map/all_to_all | solution.py:142
  326.5 415.2 %copy-start.3 = (bf16[256,256]{1,0:T(8,128)(2,1)S(1)}, bf16[256,256]{1,0:T(8,128)(2,1)}, u32[]{:S(2)}) copy-start(bf16[256,256]{1,0:T(8,128)(2,1)} %param.25) | copy-start | bytes 393220
  326.5 415.2 %copy-start.4 = (bf16[256,256]{1,0:T(8,128)(2,1)S(1)}, bf16[256,256]{1,0:T(8,128)(2,1)}, u32[]{:S(2)}) copy-start(bf16[256,256]{1,0:T(8,128)(2,1)} %param.24) | copy-start | bytes 393220
  326.5 415.2 %copy-start.5 = (bf16[256,256]{1,0:T(8,128)(2,1)S(1)}, bf16[256,256]{1,0:T(8,128)(2,1)}, u32[]{:S(2)}) copy-start(bf16[256,256]{1,0:T(8,128)(2,1)} %param.23) | copy-start | bytes 393220
  326.5 415.2 %all-gather.2.cloned.1.call-start = ((), (), s32[]{:S(2)}) async-start(), calls=%async_computation.3 | async-start | bytes 6488064 | tf_op jit(solution)/shard_map/all_gather | solution.py:151
  505.4 379.8 %reduce-scatter.2.cloned.1.call-start = ((), (), s32[]{:S(2)}) async-start(), calls=%async_computation.4 | async-start | bytes 2228224 | tf_op jit(solution)/shard_map/reduce_scatter | solution.py:153
Sparse Core Ops, SparseCore 0:
  505.5 236.1 all-gather.1
  747.8 137.2 reduce-scatter.1
where the time goes:
time: 894 us; the launch traced here: 892 us
  waiting for transfers between devices  723 us (81%)
  local copies, waits for them, and re-layouts  44.4 us (5%)
  starting transfers between devices  33.9 us (4%)
  other arithmetic  31.2 us (3%)
  matrix products  25.4 us (3%)
  loops' own time  20.1 us (2%)
  between operations  13.6 us (2%)
    all_gather x1, waiting for transfers between devices, per_device(): gradients = lax.all_gather(own_grads, 'ctx', axis=0, tiled=True)  236 us
    all_to_all x1, waiting for transfers between devices, per_device(): lax.all_to_all(part_grads.reshape(context_count, slab_rows, part_width),...  175 us
    all_to_all x1, waiting for transfers between devices, per_device(): lax.all_to_all(spread, 'ctx', 0, 0, tiled=True)  175 us
    reduce_scatter x1, waiting for transfers between devices, per_device(): lax.psum_scatter(lax.dot_general(gradients, projections, (((1,), (1,)), (...  137 us
    all_to_all x1, starting transfers between devices, per_device(): lax.all_to_all(part_grads.reshape(context_count, slab_rows, part_width),...  18 us
  transfers between devices with their start and end apart: 4, of which 4 were waited for; matrix products, arithmetic and copies ran while one was open for 0% of the time, Pallas kernels for 0%

commit v1 on v0

--- a/solution.py
+++ b/solution.py
@@ -148,7 +148,9 @@
     )
     finished = jnp.sum(arrived.astype(jnp.float32), axis=0).astype(jnp.bfloat16)
     own_grads = jnp.concatenate([local_grads, finished], axis=1)
-    gradients = lax.all_gather(own_grads, "ctx", axis=0, tiled=True)
+    gradients = jnp.concatenate(
+        lax.all_to_all(jnp.stack([own_grads] * lax.axis_size("ctx")), "ctx", 0, 0), axis=0
+    )
     projections = jnp.concatenate([w_query, w_key, w_value], axis=1)
     return lax.psum_scatter(
         lax.dot_general(

time: 894 us -> 933 us (1.044)
  blocking collectives: 0 us -> 291 us
  waiting for transfers between devices: 723 us -> 471 us
    all_to_all x0 -> x1, blocking collectives: none -> 291 us  [per_device(): lax.all_to_all(jnp.stack([own_grads] * lax.axis_size('ctx')), 'ctx', 0, 0)]
    all_gather x1 -> x0, waiting for transfers between devices: 236 us -> none  [per_device(): gradients = lax.all_gather(own_grads, 'ctx', axis=0, tiled=True)]
    reduce_scatter x1, waiting for transfers between devices: 137 us -> 122 us  [per_device(): lax.psum_scatter(lax.dot_general(gradients, projections, (((1,), (1,)), (...]
  transfers between devices with their start and end apart: 4 -> 3, of which waited for: 4 -> 3; matrix products, arithmetic and copies ran while one was open for 0% -> 0% of each run, Pallas kernels for 0% -> 0%
where the time goes in v1:
time: 933 us; the launch traced here: 931 us
  waiting for transfers between devices  471 us (50%)
  blocking collectives  291 us (31%)
  local copies, waits for them, and re-layouts  45.8 us (5%)
  starting transfers between devices  33.9 us (4%)
  other arithmetic  31.1 us (3%)
  matrix products  22.6 us (2%)
  loops' own time  22.3 us (2%)
  between operations  13.6 us (1%)
    all_to_all x1, blocking collectives, per_device(): lax.all_to_all(jnp.stack([own_grads] * lax.axis_size('ctx')), 'ctx', 0, 0)  291 us
    all_to_all x1, waiting for transfers between devices, per_device(): lax.all_to_all(part_grads.reshape(context_count, slab_rows, part_width),...  175 us
    all_to_all x1, waiting for transfers between devices, per_device(): lax.all_to_all(spread, 'ctx', 0, 0, tiled=True)  175 us
    reduce_scatter x1, waiting for transfers between devices, per_device(): lax.psum_scatter(lax.dot_general(gradients, projections, (((1,), (1,)), (...  122 us
  transfers between devices with their start and end apart: 3, of which 3 were waited for; matrix products, arithmetic and copies ran while one was open for 0% of the time, Pallas kernels for 0%

profile of v1, /device:TPU:2, one launch (start us, length us, event | category | flops | bytes accessed | tf_op | source)
XLA Modules:
  0.0 931.2 jit_solution(1967418325772480129)
XLA Ops:
  6.5 0.9 pad_maximum_fusion.1
  7.5 2.9 broadcast_in_dim.103
  10.5 15.9 %all-to-all-start = ((bf16[32,128,512]{1,2,0:T(8,128)(2,1)}), bf16[32,128,512]{1,2,0:T(8,128)(2,1)}, u32[]{:S(2)}, u32[]{:S(2)}) async-start(bf16[32,128,512]{1,2,0:T(8,128)(2,1)} %broadcast_in_dim.103), calls=%async_computation | async-start | bytes 8388608 | tf_op jit(solution)/shard_map/all_to_all | solution.py:71
  26.9 174.6 %all-to-all-done = bf16[32,128,512]{1,2,0:T(8,128)(2,1)} async-done(((bf16[32,128,512]{1,2,0:T(8,128)(2,1)}), bf16[32,128,512]{1,2,0:T(8,128)(2,1)}, u32[]{:S(2)}, u32[]{:S(2)}) %all-to-all-start) | async-done | bytes 4194336 | tf_op jit(solution)/shard_map/all_to_all | solution.py:71
  201.5 6.5 copy.66
  208.0 3.8 fusion.27
  211.9 2.1 reshape.95
  213.9 2.0 copy.74
  216.0 32.5 %while.33 = (s32[]{:T(128)}, f32[2,128]{1,0:T(2,128)S(1)}, f32[2,128]{1,0:T(2,128)S(1)}, s32[8]{0:T(128)S(1)}, s32[32,32]{1,0:T(8,128)}, /*index=5*/s32[]{:T(128...) while((s32[]{:T(128)}, f32[2,128]{1,0:T(2,128)S(1)}, ...), condition=%wide.region_6.7_spmd, body=%wide.region_0.6_spmd.sunk | while | flops 34406940 | bytes 1391623 | solution.py:94
  230.2 0.8 broadcast_reduce_fusion.4
  234.3 0.8 broadcast_reduce_fusion.4
  238.3 0.8 broadcast_reduce_fusion.4
  242.4 0.8 broadcast_reduce_fusion.4
  246.5 0.8 broadcast_reduce_fusion.4
  248.5 4.0 reshape.96
  252.4 3.3 copy.75
  255.8 56.2 %while.34 = (s32[]{:T(128)}, f32[128,2,128]{2,0,1:T(8,128)S(1)}, bf16[8,512,512]{2,1,0:T(8,128)(2,1)}, s32[8]{0:T(128)S(1)}, s32[32,32]{1,0:T(8,128)}, /*index=5...) while((s32[]{:T(128)}, f32[128,2,128]{2,0,1:T(8,128)S(1)}, ...), condition=%wide.region_13.14_spmd, body=%wide.region_8.13_spmd.sunk | while | flops 170721312 | bytes 8655399 | solution.py:134
  259.3 2.5 conditional.5
  259.7 1.2 fusion.11
  262.0 0.8 constant_dynamic-update-slice_fusion.2
  264.9 0.8 broadcast_reduce_fusion.5
  266.3 2.5 conditional.5
  266.7 1.2 fusion.11
  269.0 0.8 constant_dynamic-update-slice_fusion.2
  273.3 2.5 conditional.5
  273.8 1.2 fusion.11
  276.0 0.9 constant_dynamic-update-slice_fusion.2
  280.4 2.5 conditional.5
  280.8 1.2 fusion.11
  283.1 0.8 constant_dynamic-update-slice_fusion.2
  287.4 2.5 conditional.5
  287.8 1.2 fusion.11
  290.1 0.8 constant_dynamic-update-slice_fusion.2
  294.4 2.5 conditional.5
  294.8 1.2 fusion.11
  297.1 0.8 constant_dynamic-update-slice_fusion.2
  301.5 2.5 conditional.5
  301.9 1.2 fusion.11
  304.2 0.8 constant_dynamic-update-slice_fusion.2
  308.5 2.5 conditional.5
  308.9 1.2 fusion.11
  311.2 0.8 constant_dynamic-update-slice_fusion.2
  312.0 18.0 %all-to-all-start.1 = ((bf16[32,128,512]{2,1,0:T(8,128)(2,1)}), bf16[32,128,512]{2,1,0:T(8,128)(2,1)}, u32[]{:S(2)}, u32[]{:S(2)}) async-start(bf16[32,128,512]{2,1,0:T(8,128)(2,1)} %bitcast.67), calls=%async_computation.1 | async-start | bytes 8388608 | tf_op jit(solution)/shard_map/all_to_all | solution.py:142
  330.3 175.1 %all-to-all-done.1 = bf16[32,128,512]{2,1,0:T(8,128)(2,1)} async-done(((bf16[32,128,512]{2,1,0:T(8,128)(2,1)}), bf16[32,128,512]{2,1,0:T(8,128)(2,1)}, u32[]{:S(2)}, u32[]{:S(2)}) %all-to-all-start.1) | async-done | bytes 4194336 | tf_op jit(solution)/shard_map/all_to_all | solution.py:142
  505.3 2.8 reduce_sum.43
  508.9 290.7 %all_to_all.15 = bf16[32,128,768]{2,1,0:T(8,128)(2,1)S(1)} all-to-all(bf16[32,128,768]{2,1,0:T(8,128)(2,1)S(1)} %stack.2), channel_id=1, replica_groups=mesh['ctx'=32,'tp'=16] {'ctx'}, dimensions={0} | all-to-all | bytes 12582912 | tf_op jit(solution)/shard_map/all_to_all | solution.py:152
  799.6 3.2 convolution_convert_fusion.3
  802.8 121.6 %reduce-scatter.2.cloned.1.call-done = bf16[256,256]{1,0:T(8,128)(2,1)} async-done(((bf16[4096,256]{1,0:T(8,128)(2,1)}), bf16[256,256]{1,0:T(8,128)(2,1)}) %reduce-scatter.2.cloned.1.call-update) | async-done | bytes 131088 | tf_op jit(solution)/shard_map/reduce_scatter | solution.py:155
  (225 shorter events, 51.5 us)
Async XLA Ops:
  10.5 15.9 %copy-start.1 = (bf16[128,256]{1,0:T(8,128)(2,1)S(1)}, bf16[128,256]{1,0:T(8,128)(2,1)}, u32[]{:S(2)}) copy-start(bf16[128,256]{1,0:T(8,128)(2,1)} %param.17) | copy-start | bytes 196612
  10.5 16.2 %copy-start.2 = (bf16[128,256]{1,0:T(8,128)(2,1)S(1)}, bf16[128,256]{1,0:T(8,128)(2,1)}, u32[]{:S(2)}) copy-start(bf16[128,256]{1,0:T(8,128)(2,1)} %param.21) | copy-start | bytes 196612
  10.5 16.3 %copy-start = (bf16[128,256]{1,0:T(8,128)(2,1)S(1)}, bf16[128,256]{1,0:T(8,128)(2,1)}, u32[]{:S(2)}) copy-start(bf16[128,256]{1,0:T(8,128)(2,1)} %param.20) | copy-start | bytes 196612
  10.5 191.0 %all-to-all-start = ((bf16[32,128,512]{1,2,0:T(8,128)(2,1)}), bf16[32,128,512]{1,2,0:T(8,128)(2,1)}, u32[]{:S(2)}, u32[]{:S(2)}) async-start(bf16[32,128,512]{1,2,0:T(8,128)(2,1)} %broadcast_in_dim.103), calls=%async_computation | async-start | bytes 8388608 | tf_op jit(solution)/shard_map/all_to_all | solution.py:71
  312.0 193.3 %all-to-all-start.1 = ((bf16[32,128,512]{2,1,0:T(8,128)(2,1)}), bf16[32,128,512]{2,1,0:T(8,128)(2,1)}, u32[]{:S(2)}, u32[]{:S(2)}) async-start(bf16[32,128,512]{2,1,0:T(8,128)(2,1)} %bitcast.67), calls=%async_computation.1 | async-start | bytes 8388608 | tf_op jit(solution)/shard_map/all_to_all | solution.py:142
  330.0 594.4 %reduce-scatter.2.cloned.1.call-start = ((), (), s32[]{:S(2)}) async-start(), calls=%async_computation.4 | async-start | bytes 2228224 | tf_op jit(solution)/shard_map/reduce_scatter | solution.py:155
  508.9 290.7 %copy-start.3 = (bf16[256,256]{1,0:T(8,128)(2,1)S(1)}, bf16[256,256]{1,0:T(8,128)(2,1)}, u32[]{:S(2)}) copy-start(bf16[256,256]{1,0:T(8,128)(2,1)} %param.25) | copy-start | bytes 393220
  508.9 290.7 %copy-start.4 = (bf16[256,256]{1,0:T(8,128)(2,1)S(1)}, bf16[256,256]{1,0:T(8,128)(2,1)}, u32[]{:S(2)}) copy-start(bf16[256,256]{1,0:T(8,128)(2,1)} %param.24) | copy-start | bytes 393220
  508.9 290.7 %copy-start.5 = (bf16[256,256]{1,0:T(8,128)(2,1)S(1)}, bf16[256,256]{1,0:T(8,128)(2,1)}, u32[]{:S(2)}) copy-start(bf16[256,256]{1,0:T(8,128)(2,1)} %param.23) | copy-start | bytes 393220
Sparse Core Ops, SparseCore 0:
  802.9 121.4 reduce-scatter.1
